TPU v7x, 512 devices: a whole 4x8x8 slice. The times are simulated.
512 devices in a mesh: expert: 64 (over z, y), tensor: 8 (over x, core).
Axes of the slice: x: 4, y: 8, z: 8, core: 2. Of those that a mesh axis runs over, the one named last changes fastest.
Arguments:
- attn_out: bfloat16 [8192, 4096], P('expert', 'tensor'), may hold values from -6 to 6
- out_weight: bfloat16 [4096, 2048], P('tensor'), may hold values from -0.09375 to 0.09375
- residual: bfloat16 [8192, 2048], P(('expert', 'tensor')), may hold values from -6 to 6
- attn_gain: float32 [2048], replicated, may hold values from 0.1 to 1.9
- expert_ids: int32 [8192, 8], P('expert'), may hold values from 0 to 127, all different within a row; in each aligned block of 128 rows (0 to 127, 128 to 255, ...) at most 12 rows name the same one
- route_weights: float32 [8192, 8], P('expert'), may hold values from 0.05 to 0.3
- w_gate: bfloat16 [64, 2048, 1536], P('expert', None, 'tensor'), may hold values from -0.125 to 0.125
- w_up: bfloat16 [64, 2048, 1536], P('expert', None, 'tensor'), may hold values from -0.125 to 0.125
- w_down: bfloat16 [64, 1536, 2048], P('expert', 'tensor'), may hold values from -0.21875 to 0.21875
- input_gain: float32 [2048], replicated, may hold values from 0.1 to 1.9
- q_weight: bfloat16 [2048, 4096], P('expert', 'tensor'), may hold values from -0.125 to 0.125
- kv_weight: bfloat16 [2048, 1024], P('expert', 'tensor'), may hold values from -0.125 to 0.125
- q_gain: float32 [128], replicated, may hold values from 0.1 to 1.9
- k_gain: float32 [128], replicated, may hold values from 0.1 to 1.9
Outputs:
- next_residual: bfloat16 [8192, 2048], P(('expert', 'tensor'))
- queries: bfloat16 [8192, 4096], P('expert', 'tensor')
- keys_values: bfloat16 [8192, 1024], P('expert', 'tensor')
Inputs may be any that keep to these rules, and one draw needn't show every extreme that they name: `expert_ids`: each row names 8 different experts. In each aligned block of 128 rows no expert is named by more than 12 rows, and in some block one expert is named by exactly 12 rows.
All inputs are finite; a program needn't handle non-finite values.
Results may differ from a plain program's by a relative error of at most 0.012.
Values may be sent and summed in bfloat16 or wider, within the bound.
A program may use at most 64 MiB of HBM per device.

v0:
```python
import jax
import jax.numpy as jnp
from jax import lax
from jax.sharding import PartitionSpec as P

KV_HEADS = 4
TOP = 8


EPSILON = 1e-06


def normalize(values, gain):
    return values * lax.rsqrt(jnp.mean(values * values, axis=-1, keepdims=True) + EPSILON) * gain


def per_device(
    attn_out,
    out_weight,
    residual,
    attn_gain,
    expert_ids,
    route_weights,
    w_gate,
    w_up,
    w_down,
    input_gain,
    q_weight,
    kv_weight,
    q_gain,
    k_gain,
):
    n_expert = lax.axis_size("expert")
    n_tensor = lax.axis_size("tensor")
    share = n_tensor // 2
    tensor_index = lax.axis_index("tensor")
    group_rows = attn_out.shape[0]
    width = residual.shape[1]
    half = tensor_index // share
    capacity = 3 * group_rows * TOP // (4 * n_expert)
    all_experts = 2 * n_expert
    attn_rows = lax.psum_scatter(
        jnp.dot(attn_out, out_weight, preferred_element_type=jnp.float32),
        "tensor",
        scatter_dimension=0,
        tiled=True,
    )
    first_residual = (residual.astype(jnp.float32) + attn_rows).astype(jnp.bfloat16)
    normed = normalize(first_residual.astype(jnp.float32), attn_gain).astype(jnp.bfloat16)
    group_normed = lax.all_gather(normed, "tensor", axis=0, tiled=True)
    flat_ids = expert_ids.reshape(-1)
    onehot = (flat_ids[:, None] == jnp.arange(all_experts, dtype=jnp.int32)[None, :]).astype(
        jnp.int32
    )
    earlier = jnp.cumsum(onehot, axis=0) - onehot
    rank = jnp.sum(earlier * onehot, axis=1)
    dest = flat_ids * capacity + rank
    row_owner = jnp.arange(flat_ids.shape[0], dtype=jnp.int32) // TOP
    slot_row = jnp.full((all_experts * capacity,), group_rows, jnp.int32).at[dest].set(row_owner)
    slot_weight = (
        jnp.zeros((all_experts * capacity,), jnp.float32).at[dest].set(route_weights.reshape(-1))
    )
    own_slots = lax.dynamic_index_in_dim(
        slot_row.reshape(n_expert, 2, capacity), half, 1, keepdims=False
    )
    own_weights = lax.dynamic_index_in_dim(
        slot_weight.reshape(n_expert, 2, capacity), half, 1, keepdims=False
    )
    padded_rows = jnp.concatenate([group_normed, jnp.zeros((1, width), jnp.bfloat16)], axis=0)
    gate_w = w_gate[0]
    up_w = w_up[0]
    down_w = w_down[0]
    outgoing = jnp.take(padded_rows, own_slots, axis=0)
    arrived = lax.all_to_all(outgoing, "expert", split_axis=0, concat_axis=0, tiled=True)
    flat = arrived.reshape(-1, width)
    gate = jnp.dot(flat, gate_w, preferred_element_type=jnp.float32)
    up = jnp.dot(flat, up_w, preferred_element_type=jnp.float32)
    act = (jax.nn.silu(gate) * up).astype(jnp.bfloat16)
    part = jnp.dot(act, down_w, preferred_element_type=jnp.float32).astype(jnp.bfloat16)
    send_part = part.reshape(arrived.shape)
    returned = lax.all_to_all(send_part, "expert", split_axis=0, concat_axis=0, tiled=True)
    weighted = own_weights.reshape(-1)[:, None] * returned.reshape(-1, width).astype(jnp.float32)
    term = (
        jnp.zeros((group_rows + 1, width), jnp.float32)
        .at[own_slots.reshape(-1)]
        .add(weighted)[:group_rows]
    )
    expert_sum = lax.psum_scatter(
        term.astype(jnp.bfloat16), "tensor", scatter_dimension=0, tiled=True
    ).astype(jnp.float32)
    next_residual = (first_residual.astype(jnp.float32) + expert_sum).astype(jnp.bfloat16)
    own_normed = normalize(next_residual.astype(jnp.float32), input_gain).astype(jnp.bfloat16)
    next_normed = lax.all_gather(own_normed, "tensor", axis=0, tiled=True)
    query_cols = q_weight.shape[1]
    kv_cols = kv_weight.shape[1]
    query_raw = jnp.dot(
        next_normed,
        lax.all_gather(q_weight, "expert", axis=0, tiled=True),
        preferred_element_type=jnp.float32,
    )
    kv_raw = jnp.dot(
        next_normed,
        lax.all_gather(kv_weight, "expert", axis=0, tiled=True),
        preferred_element_type=jnp.float32,
    )
    head_size = q_gain.shape[0]
    queries = (
        normalize(query_raw.reshape(group_rows, -1, head_size), q_gain)
        .reshape(group_rows, query_cols)
        .astype(jnp.bfloat16)
    )
    heads_here = kv_cols // head_size
    head_number = tensor_index * heads_here + jnp.arange(heads_here, dtype=jnp.int32)
    is_key = head_number < KV_HEADS
    kv_shaped = kv_raw.reshape(group_rows, heads_here, head_size)
    keys_values = (
        jnp.where(is_key[None, :, None], normalize(kv_shaped, k_gain), kv_shaped)
        .reshape(group_rows, kv_cols)
        .astype(jnp.bfloat16)
    )
    return (next_residual, queries, keys_values)


def solution(mesh):
    return jax.shard_map(
        per_device,
        mesh=mesh,
        in_specs=(
            P("expert", "tensor"),
            P("tensor", None),
            P(("expert", "tensor"), None),
            P(),
            P("expert", None),
            P("expert", None),
            P("expert", None, "tensor"),
            P("expert", None, "tensor"),
            P("expert", "tensor", None),
            P(),
            P("expert", "tensor"),
            P("expert", "tensor"),
            P(),
            P(),
        ),
        out_specs=(P(("expert", "tensor"), None), P("expert", "tensor"), P("expert", "tensor")),
        check_vma=False,
    )
```

profile of v0, /device:TPU:1, one launch (start us, length us, event | category | flops | bytes accessed | tf_op | source)
XLA Modules:
  0.0 471.5 jit_solution(3789116620057749564)
XLA Ops:
  8.1 1.5 copy-done
  9.6 2.3 fusion.42
  13.4 4.3 scatter_custom_fusion
  18.4 0.7 fusion.40
  19.3 34.3 %reduce-scatter.3.cloned.1.call-done = f32[16,2048]{1,0:T(8,128)} async-done(((f32[128,2048]{1,0:T(8,128)}), f32[16,2048]{1,0:T(8,128)}) %reduce-scatter.3.cloned.1.call-update) | async-done | bytes 131088 | tf_op jit(solution)/shard_map/reduce_scatter | solution.py:42
  53.6 1.0 fusion.26
  54.7 15.1 %all_gather.12 = bf16[128,2048]{1,0:T(8,128)(2,1)S(1)} all-gather(bf16[16,2048]{1,0:T(8,128)(2,1)S(1)} %fusion.28), channel_id=1, replica_groups=mesh['expert'=64,'tensor'=8] {'tensor'}, dimensions={0}, use_global_device_ids=true | all-gather | bytes 589824 | tf_op jit(solution)/shard_map/all_gather | solution.py:50
  69.9 4.3 gather_fusion
  74.2 6.1 %reshape.208 = bf16[64,12,2048]{2,1,0:T(8,128)(2,1)} reshape(bf16[768,2048]{1,0:T(8,128)(2,1)} %gather_fusion) | data formatting | bytes 6291456 | tf_op jit(solution)/shard_map/jit(_take)/gather | solution.py:73
  80.3 2.6 broadcast_select_fusion
  82.9 108.5 %all_to_all.10 = bf16[64,12,2048]{2,1,0:T(8,128)(2,1)} all-to-all(bf16[64,12,2048]{2,1,0:T(8,128)(2,1)S(1)} %broadcast_select_fusion), channel_id=1, replica_groups=mesh['expert'=64,'tensor'=8] {'expert'}, dimensions={0} | all-to-all | bytes 6291456 | tf_op jit(solution)/shard_map/all_to_all | solution.py:74
  191.4 6.2 %reshape.204 = bf16[768,2048]{1,0:T(8,128)(2,1)} reshape(bf16[64,12,2048]{2,1,0:T(8,128)(2,1)} %all_to_all.10) | data formatting | bytes 6291456 | tf_op jit(solution)/shard_map/reshape | solution.py:75
  197.6 3.3 fusion.7
  200.8 6.5 %convolution_convert_fusion = bf16[768,2048]{1,0:T(8,128)(2,1)} fusion(bf16[768,2048]{1,0:T(8,128)(2,1)} %reshape.204, bf16[1,192,2048]{2,1,0:T(8,128)(2,1)} %param.22, bf16[1,2048,192]{1,2,0:T(8,128)(2,1)} %param.21, f32[768,192]{0,1:T(8,128)S(1)} %fusion.7), kind=kOutput, calls=%fused_computation.7 | convolution fusion | flops 1210417152 | bytes 8454144 | tf_op jit(solution)/shard_map/dot_general | solution.py:79
  207.3 6.1 %reshape.205 = bf16[64,12,2048]{2,1,0:T(8,128)(2,1)} reshape(bf16[768,2048]{1,0:T(8,128)(2,1)} %convolution_convert_fusion) | data formatting | bytes 6291456 | tf_op jit(solution)/shard_map/reshape | solution.py:80
  213.4 13.5 %all-to-all-start.1 = ((bf16[64,12,2048]{2,1,0:T(8,128)(2,1)}), bf16[64,12,2048]{2,1,0:T(8,128)(2,1)}, u32[]{:S(2)}, u32[]{:S(2)}) async-start(bf16[64,12,2048]{2,1,0:T(8,128)(2,1)} %reshape.205), calls=%async_computation.2 | async-start | bytes 8388608 | tf_op jit(solution)/shard_map/all_to_all | solution.py:81
  227.2 4.5 scatter_custom_fusion.1
  232.1 96.9 %all-to-all-done.1 = bf16[64,12,2048]{2,1,0:T(8,128)(2,1)} async-done(((bf16[64,12,2048]{2,1,0:T(8,128)(2,1)}), bf16[64,12,2048]{2,1,0:T(8,128)(2,1)}, u32[]{:S(2)}, u32[]{:S(2)}) %all-to-all-start.1) | async-done | bytes 3145760 | tf_op jit(solution)/shard_map/all_to_all | solution.py:81
  329.0 6.7 %reshape.206 = f32[768,2048]{1,0:T(8,128)} reshape(bf16[64,12,2048]{2,1,0:T(8,128)(2,1)} %all-to-all-done.1) | data formatting | bytes 9437184 | tf_op jit(solution)/shard_map/convert_element_type | solution.py:82
  335.7 15.8 %scatter_custom_fusion.2 = f32[129,2048]{1,0:T(8,128)S(1)} fusion(s32[768]{0:T(1024)S(1)} %fusion.37, f32[768,2048]{1,0:T(8,128)} %reshape.206, f32[768]{0:T(1024)S(1)} %mul.130, f32[]{:T(128)} %constant.76.clone.1), kind=kCustom, calls=%fused_computation.4 | custom fusion | flops 3145728 | bytes 7352324 | tf_op jit(solution)/shard_map/scatter-add | solution.py:86
  351.5 0.9 slice.20
  352.4 0.5 all-gather.2.cloned.1.call-update
  353.0 62.3 %all_gather.15 = bf16[2048,128]{1,0:T(8,128)(2,1)S(1)} all-gather(bf16[32,128]{1,0:T(8,128)(2,1)S(1)} %copy-done.4), channel_id=1, replica_groups=mesh['expert'=64,'tensor'=8] {'expert'}, dimensions={0}, use_global_device_ids=true | all-gather | bytes 532480 | tf_op jit(solution)/shard_map/all_gather | solution.py:103
  415.4 1.0 fusion.23
  416.5 26.1 %all_gather.13 = bf16[128,2048]{1,0:T(8,128)(2,1)S(1)} all-gather(bf16[16,2048]{1,0:T(8,128)(2,1)S(1)} %fusion.25), channel_id=1, replica_groups=mesh['expert'=64,'tensor'=8] {'tensor'}, dimensions={0}, use_global_device_ids=true | all-gather | bytes 589824 | tf_op jit(solution)/shard_map/all_gather | solution.py:93
  442.6 12.2 %all-gather.2.cloned.1.call-done = bf16[2048,512]{1,0:T(8,128)(2,1)} async-done(((bf16[32,512]{1,0:T(8,128)(2,1)}), bf16[2048,512]{1,0:T(8,128)(2,1)}) %all-gather.2.cloned.1.call-update) | async-done | bytes 2097168 | tf_op jit(solution)/shard_map/all_gather | solution.py:98
  454.8 2.8 fusion.41
  457.5 1.7 mul.146
  459.3 1.8 reduce_sum.51
  461.1 0.9 add_rsqrt_fusion
  462.4 0.7 copy.41
  463.3 0.7 fusion.21
  (64 shorter events, 3.9 us)
Async XLA Ops:
  8.0 1.6 copy-start
  8.0 4.0 copy-start.3
  8.0 45.6 %reduce-scatter.3.cloned.1.call-start = ((), (), s32[]{:S(2)}) async-start(), calls=%async_computation.4 | async-start | bytes 1179648 | tf_op jit(solution)/shard_map/reduce_scatter | solution.py:42
  11.9 41.7 %copy-start.2 = (bf16[16,2048]{1,0:T(8,128)(2,1)S(1)}, bf16[16,2048]{1,0:T(8,128)(2,1)}, u32[]{:S(2)}) copy-start(bf16[16,2048]{1,0:T(8,128)(2,1)} %param.16) | copy-start | bytes 196612
  11.9 42.7 %copy-start.5 = (f32[2048]{0:T(1024)S(1)}, f32[2048]{0:T(1024)}, u32[]{:S(2)}) copy-start(f32[2048]{0:T(1024)} %param.17) | copy-start | bytes 24580
  213.4 13.7 %copy-start.7 = (f32[128,8]{0,1:T(8,128)S(1)}, f32[128,8]{0,1:T(8,128)}, u32[]{:S(2)}) copy-start(f32[128,8]{0,1:T(8,128)} %param.19) | copy-start | bytes 12292
  213.4 115.6 %all-to-all-start.1 = ((bf16[64,12,2048]{2,1,0:T(8,128)(2,1)}), bf16[64,12,2048]{2,1,0:T(8,128)(2,1)}, u32[]{:S(2)}, u32[]{:S(2)}) async-start(bf16[64,12,2048]{2,1,0:T(8,128)(2,1)} %reshape.205), calls=%async_computation.2 | async-start | bytes 8388608 | tf_op jit(solution)/shard_map/all_to_all | solution.py:81
  226.9 188.5 %reduce-scatter.5.cloned.1.call-start = ((), (), s32[]{:S(2)}) async-start(), calls=%async_computation.5 | async-start | bytes 589824 | tf_op jit(solution)/shard_map/reduce_scatter | solution.py:88
  335.7 17.3 %copy-start.4 = (bf16[32,128]{1,0:T(8,128)(2,1)S(1)}, bf16[32,128]{1,0:T(8,128)(2,1)}, u32[]{:S(2)}) copy-start(bf16[32,128]{1,0:T(8,128)(2,1)} %param.25) | copy-start | bytes 24580
  335.7 79.6 %copy-start.9 = (f32[128]{0:T(128)S(1)}, f32[128]{0:T(128)}, u32[]{:S(2)}) copy-start(f32[128]{0:T(128)} %param.26) | copy-start | bytes 1540
  335.7 80.7 %copy-start.6 = (f32[2048]{0:T(1024)S(1)}, f32[2048]{0:T(1024)}, u32[]{:S(2)}) copy-start(f32[2048]{0:T(1024)} %param.23) | copy-start | bytes 24580
  352.4 102.4 %all-gather.2.cloned.1.call-start = ((), (), s32[]{:S(2)}) async-start(), calls=%async_computation.6 | async-start | bytes 2129920 | tf_op jit(solution)/shard_map/all_gather | solution.py:98
  415.3 47.0 %copy-start.8 = (f32[128]{0:T(128)S(1)}, f32[128]{0:T(128)}, u32[]{:S(2)}) copy-start(f32[128]{0:T(128)} %param.27) | copy-start | bytes 1540
  416.3 47.0 %copy-start.1 = (bf16[16,2048]{1,0:T(8,128)(2,1)}, bf16[16,2048]{1,0:T(8,128)(2,1)S(1)}, u32[]{:S(2)}) copy-start(bf16[16,2048]{1,0:T(8,128)(2,1)S(1)} %get-tuple-element.16) | copy-start | bytes 196612
Sparse Core Ops, SparseCore 0:
  12.1 41.4 reduce-scatter.2
  352.5 55.7 reduce-scatter.4
Sparse Core Ops, SparseCore 1:
  355.9 98.8 all-gather.1
where the time goes:
time: 476 us; the launch traced here: 471 us
  blocking collectives  212 us (45%)
  waiting for transfers between devices  144 us (30%)
  local copies, waits for them, and re-layouts  46 us (10%)
  other arithmetic  24.7 us (5%)
  between operations  15.8 us (3%)
  matrix products  15.2 us (3%)
  starting transfers between devices  13.6 us (3%)
    all_to_all x1, blocking collectives, per_device(): lax.all_to_all(outgoing, 'expert', split_axis=0, concat_axis=0, tiled=True)  108 us
    all_to_all x1, waiting for transfers between devices, per_device(): lax.all_to_all(send_part, 'expert', split_axis=0, concat_axis=0, tiled=True)  96.9 us
    all_gather x1, blocking collectives, per_device(): lax.all_gather(kv_weight, 'expert', axis=0, tiled=True)  62.3 us
    reduce_scatter x1, waiting for transfers between devices, per_device(): lax.psum_scatter(jnp.dot(attn_out, out_weight, preferred_element_type=jnp...  34.3 us
    all_gather x1, blocking collectives, per_device(): next_normed = lax.all_gather(own_normed, 'tensor', axis=0, tiled=True)  26.1 us
    scatter-add x1, other arithmetic, per_device(): term = jnp.zeros((group_rows + 1, width), jnp.float32).at[own_slots.resha...  15.8 us
    all_gather x1, blocking collectives, per_device(): group_normed = lax.all_gather(normed, 'tensor', axis=0, tiled=True)  15.1 us
    all_to_all x1, starting transfers between devices, per_device(): lax.all_to_all(send_part, 'expert', split_axis=0, concat_axis=0, tiled=True)  13.5 us
  transfers between devices with their start and end apart: 4, of which 3 were waited for; matrix products, arithmetic and copies ran while one was open for 3% of the time, Pallas kernels for 0%

commit v1 on v0

v1 whole, which is shorter than its diff:
```python
import jax
import jax.numpy as jnp
from jax import lax
from jax.experimental import pallas as pl
from jax.experimental.pallas import tpu as pltpu
from jax.sharding import PartitionSpec as P

MESH = pl.DeviceIdType.MESH
BF = jnp.bfloat16
F32 = jnp.float32

KV_HEADS = 4
TOP = 8
EPSILON = 1e-06

D = 2048
GROUP = 128
TOKENS = 16
CAP = 12
QUARTER = 512
HIDDEN = 192
PAIR_HIDDEN = 384
ROWS = 384
SLOTS = 768
QKV = 640
HEAD = 128


def normalize(values, gain):
    return values * lax.rsqrt(jnp.mean(values * values, axis=-1, keepdims=True) + EPSILON) * gain


def dot(a, b):
    return jnp.dot(a, b, preferred_element_type=F32)


def iota(shape, axis):
    return lax.broadcasted_iota(jnp.int32, shape, axis)


def kernel(
    attn_hbm,
    ow_hbm,
    res_ref,
    attn_gain,
    ids_ref,
    rw_ref,
    wg_hbm,
    wu_hbm,
    wd_hbm,
    input_gain,
    qw_hbm,
    kvw_hbm,
    q_gain,
    k_gain,
    next_ref,
    queries_ref,
    kv_ref,
    attn,
    ow,
    wg,
    wu,
    wgp,
    wup,
    wgu,
    wd_own,
    wd,
    qw,
    partial,
    rs_in,
    normed_out,
    normed_in,
    pick,
    mix_hi,
    mix_lo,
    tx,
    r1,
    x0,
    x1,
    c0,
    c1,
    hidden,
    act,
    act_in,
    y_acc,
    y0,
    y1,
    r3,
    r4,
    sums_out,
    sums_in,
    first,
    nx,
    load_sem,
    rs_send,
    rs_recv,
    nb_send,
    nb_recv,
    pair_send,
    pair_recv,
    wd_send,
    wd_recv,
    q1_send,
    q1_recv,
    q2_send,
    q2_recv,
    d1_send,
    d1_recv,
    d2_send,
    d2_recv0,
    d2_recv1,
    c_send,
    c_recv0,
    c_recv1,
    act_send,
    act_recv,
    r3_send,
    r3_recv,
    r4_send,
    r4_recv,
    sums_send,
    sums_recv,
    nx_send,
    nx_recv,
):
    e = lax.axis_index("expert")
    t = lax.axis_index("tensor")
    z, y = e // 8, e % 8
    core = t % 2
    side = (t // 2) % 2
    parity = t // 4
    partner = t + 1 - 2 * core
    cross = t + 2 - 4 * side
    core0, core1 = t - core, t - core + 1
    half = z // 4
    a = y + core * (z - y)
    b = z + core * (y - z)

    def at(first_axis, second_axis):
        return (second_axis + core * (first_axis - second_axis)) * 8 + (
            first_axis + core * (second_axis - first_axis)
        )

    def step_of(i):
        return jnp.where(i % 2 == 1, (i + 1) // 2, 8 - i // 2)

    def remote(src, dst, send, recv, expert, tensor):
        return pltpu.make_async_remote_copy(
            src_ref=src,
            dst_ref=dst,
            send_sem=send,
            recv_sem=recv,
            device_id={"expert": expert, "tensor": tensor},
            device_id_type=MESH,
        )

    def arrived(dst, send, recv):
        remote(dst, dst, send, recv, e, partner).wait_recv()

    def left(src, send, recv):
        remote(src, src, send, recv, e, partner).wait_send()

    barrier = pltpu.get_barrier_semaphore()

    @pl.loop(1, 8)
    def _(i):
        pl.semaphore_signal(
            barrier, inc=1, device_id={"expert": e, "tensor": (t + i) % 8}, device_id_type=MESH
        )
        for which in (core0, core1):
            pl.semaphore_signal(
                barrier,
                inc=1,
                device_id={"expert": z * 8 + (y + i) % 8, "tensor": which},
                device_id_type=MESH,
            )
            pl.semaphore_signal(
                barrier,
                inc=1,
                device_id={"expert": ((z + i) % 8) * 8 + y, "tensor": which},
                device_id_type=MESH,
            )

    loads = [
        pltpu.make_async_copy(attn_hbm, attn, load_sem.at[0]),
        pltpu.make_async_copy(ow_hbm, ow, load_sem.at[1]),
        pltpu.make_async_copy(qw_hbm, qw.at[b, a, :, pl.ds(0, 512)], load_sem.at[2]),
        pltpu.make_async_copy(kvw_hbm, qw.at[b, a, :, pl.ds(512, 128)], load_sem.at[3]),
        pltpu.make_async_copy(wg_hbm.at[0], wg, load_sem.at[4]),
        pltpu.make_async_copy(wu_hbm.at[0], wu, load_sem.at[5]),
        pltpu.make_async_copy(wd_hbm.at[0], wd_own, load_sem.at[6]),
    ]
    for load in loads:
        load.start()

    loads[0].wait()
    loads[1].wait()
    for n in range(4):
        cols = slice(n * 512, n * 512 + 512)
        partial[:, :, cols] = dot(attn[...], ow[:, cols]).astype(BF).reshape(8, TOKENS, 512)

    pl.semaphore_wait(barrier, 35)

    @pl.loop(1, 8)
    def _(i):
        d = (t + i) % 8
        remote(partial.at[d], rs_in.at[t], rs_send.at[d], rs_recv.at[t], e, d).start()

    loads[2].wait()
    loads[3].wait()

    @pl.loop(1, 8)
    def _(i):
        d = (a + step_of(i)) % 8
        remote(
            qw.at[b, a], qw.at[b, a], q1_send.at[d], q1_recv.at[a], at(d, b), t
        ).start()

    loads[4].wait()
    remote(wg, wgp, pair_send.at[0], pair_recv.at[0], e, partner).start()
    loads[5].wait()
    remote(wu, wup, pair_send.at[1], pair_recv.at[1], e, partner).start()

    position = iota((GROUP, 64), 1)
    p_first, p_second = position // 8, position % 8
    expert_of = 2 * at(p_first, p_second) + parity
    ids = ids_ref[...]
    weights = rw_ref[...]
    named = jnp.zeros((GROUP, 64), F32)
    weight_of = jnp.zeros((GROUP, 64), F32)
    for k in range(TOP):
        hit = expert_of == ids[:, k : k + 1]
        named += jnp.where(hit, 1.0, 0.0)
        weight_of += jnp.where(hit, weights[:, k : k + 1], 0.0)
    lower = jnp.where(iota((GROUP, GROUP), 1) < iota((GROUP, GROUP), 0), 1.0, 0.0).astype(BF)
    rank = dot(lower, named.astype(BF))
    code = (named * (rank + 1.0)).astype(BF)
    slot = iota((64, SLOTS), 1)
    start = iota((64, SLOTS), 0) * CAP
    spread = jnp.where((slot >= start) & (slot < start + CAP), 1.0, 0.0).astype(BF)
    wanted = (iota((GROUP, SLOTS), 1) % CAP + 1).astype(F32)
    chosen = dot(code, spread) == wanted
    high = weight_of.astype(BF)
    low = (weight_of - high.astype(F32)).astype(BF)
    mix_hi[...] = jnp.where(chosen, dot(high, spread), 0.0).astype(BF)
    mix_lo[...] = jnp.where(chosen, dot(low, spread), 0.0).astype(BF)
    pick[...] = jnp.where(chosen, 1.0, 0.0).T.astype(BF)

    after, before = at(a, (b + 1) % 8), at(a, (b + 7) % 8)

    def ring(step):
        rows = ((b + 8 - step) % 8, (b + step) % 8)
        if step == 3:
            pieces = (qw.at[rows[0], pl.ds(0, 4)], qw.at[rows[1], pl.ds(4, 4)])
        else:
            pieces = (qw.at[rows[0]], qw.at[rows[1]])
        return [
            remote(pieces[k], pieces[k], q2_send.at[step, k], q2_recv.at[step, k], (after, before)[k], t)
            for k in range(2)
        ]

    def ring_wait(step):
        rows = ((b + 7 - step) % 8, (b + 1 + step) % 8)
        if step == 3:
            pieces = (qw.at[rows[0], pl.ds(0, 4)], qw.at[rows[1], pl.ds(4, 4)])
        else:
            pieces = (qw.at[rows[0]], qw.at[rows[1]])
        for k in range(2):
            arrived(pieces[k], q2_send.at[step, k], q2_recv.at[step, k])

    @pl.loop(1, 8)
    def _(i):
        s = (a + i) % 8
        arrived(qw.at[b, s], q1_send.at[s], q1_recv.at[s])

    for c in ring(0):
        c.start()

    rs_in[t] = partial[t]

    @pl.loop(1, 8)
    def _(i):
        s = (t + i) % 8
        arrived(rs_in.at[s], rs_send.at[s], rs_recv.at[s])

    total = res_ref[...].astype(F32)
    attn_sum = rs_in[0].astype(F32)
    for k in range(1, 8):
        attn_sum += rs_in[k].astype(F32)
    first_residual = (total + attn_sum).astype(BF)
    first[...] = first_residual
    normed = normalize(first_residual.astype(F32), attn_gain[...]).astype(BF)
    for s in range(4):
        normed_out[s] = normed[:, s * QUARTER : s * QUARTER + QUARTER]
    normed_in[t] = normed_out[t % 4]

    @pl.loop(1, 8)
    def _(i):
        d = (t + i) % 8
        remote(normed_out.at[d % 4], normed_in.at[t], nb_send.at[d], nb_recv.at[t], e, d).start()

    loads[6].wait()
    own_half = pl.ds(pl.multiple_of(side * 1024, 1024), 1024)
    other_half = pl.ds(pl.multiple_of((1 - side) * 1024, 1024), 1024)
    remote(wd_own.at[:, own_half], wd.at[1], wd_send.at[0], wd_recv.at[0], e, partner).start()
    remote(wd_own.at[:, other_half], wd.at[2], wd_send.at[1], wd_recv.at[1], e, cross).start()
    wd[0] = wd_own[:, own_half]

    ring_wait(0)
    for c in ring(1):
        c.start()

    @pl.loop(1, 8)
    def _(i):
        s = (t + i) % 8
        arrived(normed_in.at[s], nb_send.at[s], nb_recv.at[s])

    group = normed_in[...].reshape(GROUP, QUARTER)
    for k in range(4):
        rows = slice(k * 192, k * 192 + 192)
        tx[2 * k : 2 * k + 2] = (
            dot(pick[rows, :], group).astype(BF).reshape(2, 8, 3, 4, QUARTER)
        )

    @pl.loop(1, 8)
    def _(i):
        d = (a + step_of(i)) % 8
        remote(tx.at[d], r1.at[a], d1_send, d1_recv, at(d, b), t).start()

    keep = pltpu.make_async_copy(tx.at[a], r1.at[a], d1_recv)
    keep.start()

    arrived(wgp, pair_send.at[0], pair_recv.at[0])
    arrived(wup, pair_send.at[1], pair_recv.at[1])

    @pl.loop(0, 16)
    def _(i):
        rows = pl.ds(pl.multiple_of(i * 128, 128), 128)
        wgu[rows, 0:PAIR_HIDDEN] = jnp.concatenate([wg[rows, :], wgp[rows, :]], axis=1)
        wgu[rows, PAIR_HIDDEN : 2 * PAIR_HIDDEN] = jnp.concatenate(
            [wu[rows, :], wup[rows, :]], axis=1
        )

    arrived(wd.at[2], wd_send.at[1], wd_recv.at[1])
    remote(wd.at[2], wd.at[3], wd_send.at[2], wd_recv.at[2], e, partner).start()

    arrived(r1, d1_send, d1_recv)

    def to_core0_path(d):
        return r1.at[:, d], x0.at[z % 4], d2_recv0.at[z % 4]

    def to_core1_path(d, hf):
        return r1.at[4 * hf : 4 * hf + 4, d], x1.at[y], d2_recv1.at[y]

    @pl.when(core == 0)
    def _():
        @pl.loop(1, 8)
        def _(i):
            d = (b + step_of(i)) % 8
            src, dst, sem = to_core0_path(d)
            remote(src, dst, d2_send, sem, at(a, d), core0 + half).start()

        src, dst, sem = to_core0_path(b)

        @pl.when(half == 0)
        def _():
            pltpu.make_async_copy(src, dst, sem).start()

        @pl.when(half == 1)
        def _():
            remote(src, dst, d2_send, sem, e, core1).start()

    @pl.when(core == 1)
    def _():
        @pl.loop(1, 8)
        def _(i):
            d = (b + step_of(i)) % 8
            for hf in range(2):
                src, dst, sem = to_core1_path(d, hf)
                remote(src, dst, d2_send, sem, at(a, d), core0 + hf).start()

        src, dst, sem = to_core1_path(b, 0)
        remote(src, dst, d2_send, sem, e, core0).start()
        src, dst, sem = to_core1_path(b, 1)
        pltpu.make_async_copy(src, dst, sem).start()

    @pl.loop(0, 4)
    def _(i):
        for j in range(2):
            k = (y + step_of(2 * i + j)) % 8
            arrived(x1.at[k], c_send, d2_recv1.at[k])
            remote(x1.at[k], c1.at[k], c_send, c_recv1.at[k], e, cross).start()
        arrived(x0.at[i], c_send, d2_recv0.at[i])
        remote(x0.at[i], c0.at[i], c_send, c_recv0.at[i], e, cross).start()

    ring_wait(1)
    for c in ring(2):
        c.start()

    def multiply(rows_of, column, zero):
        rows = pl.ds(pl.multiple_of(column, QUARTER), QUARTER)
        values = rows_of()
        for n in range(3):
            cols = slice(n * 256, n * 256 + 256)
            product = dot(values, wgu[rows, cols])
            hidden[:, cols] = product if zero else hidden[:, cols] + product

    def natural(ref):
        return lambda: ref[...].reshape(ROWS, QUARTER)

    def turned(ref):
        return lambda: jnp.concatenate(
            [ref[:, k].reshape(96, QUARTER) for k in range(4)], axis=0
        )

    multiply(natural(x0), side * 1024, True)
    multiply(turned(x1), side * 1024 + QUARTER, False)

    @pl.loop(0, 4)
    def _(i):
        arrived(c0.at[i], c_send, c_recv0.at[i])

    multiply(natural(c0), (1 - side) * 1024, False)

    @pl.loop(0, 8)
    def _(i):
        arrived(c1.at[i], c_send, c_recv1.at[i])

    multiply(turned(c1), (1 - side) * 1024 + QUARTER, False)

    gate = hidden[:, 0:PAIR_HIDDEN]
    act[...] = (
        gate * (1.0 / (1.0 + jnp.exp(-gate))) * hidden[:, PAIR_HIDDEN : 2 * PAIR_HIDDEN]
    ).astype(BF)
    remote(act, act_in, act_send, act_recv, e, cross).start()

    ring_wait(2)
    for c in ring(3):
        c.start()

    arrived(wd.at[1], wd_send.at[0], wd_recv.at[0])
    arrived(wd.at[3], wd_send.at[2], wd_recv.at[2])
    for n in range(4):
        cols = slice(n * 256, n * 256 + 256)
        y_acc[:, cols] = dot(act[...], wd[0:2, :, cols].reshape(PAIR_HIDDEN, 256))
    arrived(act_in, act_send, act_recv)
    for n in range(4):
        cols = slice(n * 256, n * 256 + 256)
        out = y_acc[:, cols] + dot(act_in[...], wd[2:4, :, cols].reshape(PAIR_HIDDEN, 256))
        blocks = out.astype(BF).reshape(4, 8, 3, 4, 256)
        into = slice((n % 2) * 256, (n % 2) * 256 + 256)
        if n < 2:
            y0[:, :, :, :, into] = blocks
        else:
            for k in range(4):
                y1[:, k, :, :, into] = blocks[k]

    first_zone = 4 * core

    @pl.loop(0, 4)
    def _(i):
        zone = first_zone + i
        src, dst = y0.at[i], r3.at[z]

        @pl.when(zone != z)
        def _():
            remote(src, dst, r3_send, r3_recv, zone * 8 + y, core0).start()

        @pl.when((zone == z) & (core == 0))
        def _():
            pltpu.make_async_copy(src, dst, r3_recv).start()

        @pl.when((zone == z) & (core == 1))
        def _():
            remote(src, dst, r3_send, r3_recv, e, core0).start()

    @pl.loop(1, 8)
    def _(i):
        d = (y + step_of(i)) % 8
        remote(
            y1.at[d], r3.at[y, pl.ds(first_zone, 4)], r3_send, r3_recv, z * 8 + d, core1
        ).start()

    @pl.when(core == 1)
    def _():
        pltpu.make_async_copy(y1.at[y], r3.at[y, pl.ds(first_zone, 4)], r3_recv).start()

    @pl.when(core == 0)
    def _():
        remote(y1.at[y], r3.at[y, pl.ds(first_zone, 4)], r3_send, r3_recv, e, core1).start()

    arrived(r3, r3_send, r3_recv)

    @pl.loop(1, 8)
    def _(i):
        d = (a + step_of(i)) % 8
        remote(r3.at[:, d], r4.at[a], r4_send, r4_recv, at(d, b), t).start()

    pltpu.make_async_copy(r3.at[:, a], r4.at[a], r4_recv).start()
    arrived(r4, r4_send, r4_recv)

    returned = r4[...].reshape(SLOTS, QUARTER)
    weighted = dot(mix_hi[...], returned) + dot(mix_lo[...], returned)
    sums_out[...] = weighted.astype(BF).reshape(8, TOKENS, QUARTER)
    sums_in[t] = sums_out[t]

    @pl.loop(1, 8)
    def _(i):
        d = (t + i) % 8
        remote(sums_out.at[d], sums_in.at[t], sums_send.at[d], sums_recv.at[t], e, d).start()

    @pl.loop(1, 8)
    def _(i):
        s = (t + i) % 8
        arrived(sums_in.at[s], sums_send.at[s], sums_recv.at[s])

    expert_sum = jnp.concatenate(
        [sums_in[s].astype(F32) + sums_in[s + 4].astype(F32) for s in range(4)], axis=1
    )
    next_residual = (first[...].astype(F32) + expert_sum).astype(BF)
    next_ref[...] = next_residual
    nx[t] = normalize(next_residual.astype(F32), input_gain[...]).astype(BF)

    @pl.loop(1, 8)
    def _(i):
        d = (t + i) % 8
        remote(nx.at[t], nx.at[t], nx_send.at[d], nx_recv.at[t], e, d).start()

    ring_wait(3)

    @pl.loop(1, 8)
    def _(i):
        s = (t + i) % 8
        arrived(nx.at[s], nx_send.at[s], nx_recv.at[s])

    tokens = nx[...].reshape(GROUP, D)
    raw = jnp.zeros((GROUP, QKV), F32)
    for zz in range(8):
        blocks = []
        for yy in range(8):
            second = zz + core * (yy - zz)
            blocks.append(qw[second, yy + core * (zz - yy)])
        raw += dot(tokens[:, zz * 256 : zz * 256 + 256], jnp.concatenate(blocks, axis=0))
    for head in range(4):
        cols = slice(head * HEAD, head * HEAD + HEAD)
        queries_ref[:, cols] = normalize(raw[:, cols], q_gain[...]).astype(BF)
    kv_raw = raw[:, 512:QKV]
    kv_ref[...] = jnp.where(t < KV_HEADS, normalize(kv_raw, k_gain[...]), kv_raw).astype(BF)

    @pl.loop(1, 8)
    def _(i):
        d = (t + i) % 8
        left(partial.at[d], rs_send.at[d], rs_recv.at[d])
        left(normed_out.at[0], nb_send.at[d], nb_recv.at[d])
        left(sums_out.at[d], sums_send.at[d], sums_recv.at[d])
        left(nx.at[t], nx_send.at[d], nx_recv.at[d])
        n = (a + i) % 8
        left(qw.at[b, a], q1_send.at[n], q1_recv.at[n])

    left(wg, pair_send.at[0], pair_recv.at[0])
    left(wu, pair_send.at[1], pair_recv.at[1])
    left(wd.at[0], wd_send.at[0], wd_recv.at[0])
    left(wd.at[0], wd_send.at[1], wd_recv.at[1])
    left(wd.at[0], wd_send.at[2], wd_recv.at[2])
    for step in range(4):
        for c in ring(step):
            c.wait_send()
    left(tx.at[0:7], d1_send, d1_recv)
    left(act, act_send, act_recv)
    left(r4.at[0:7], r4_send, r4_recv)
    left(x0, c_send, c_recv0.at[0])
    left(x1, c_send, c_recv0.at[0])

    @pl.when(core == 0)
    def _():
        left(r1.at[0:7], d2_send, d2_recv0.at[0])

        @pl.when(half == 1)
        def _():
            left(r1.at[0], d2_send, d2_recv0.at[0])

    @pl.when(core == 1)
    def _():
        left(r1.at[0:7], d2_send, d2_recv0.at[0])
        left(r1.at[0, 0:4], d2_send, d2_recv0.at[0])

    left(y1.at[0:7], r3_send, r3_recv)

    @pl.when((core == 0) & (half == 0))
    def _():
        left(y0.at[0:3], r3_send, r3_recv)
        left(y1.at[0], r3_send, r3_recv)

    @pl.when((core == 0) & (half == 1))
    def _():
        left(y0, r3_send, r3_recv)
        left(y1.at[0], r3_send, r3_recv)

    @pl.when(core == 1)
    def _():
        left(y0, r3_send, r3_recv)


def per_device(
    attn_out,
    out_weight,
    residual,
    attn_gain,
    expert_ids,
    route_weights,
    w_gate,
    w_up,
    w_down,
    input_gain,
    q_weight,
    kv_weight,
    q_gain,
    k_gain,
):
    any_spec = pl.BlockSpec(memory_space=pl.ANY)
    vmem = pl.BlockSpec(memory_space=pltpu.VMEM)
    dma = pltpu.SemaphoreType.DMA
    rows = (3, 4, QUARTER)

    def buf(*shape):
        return pltpu.VMEM(shape, BF)

    return pl.pallas_call(
        kernel,
        out_shape=(
            jax.ShapeDtypeStruct((TOKENS, D), BF),
            jax.ShapeDtypeStruct((GROUP, 512), BF),
            jax.ShapeDtypeStruct((GROUP, HEAD), BF),
        ),
        in_specs=[
            any_spec,
            any_spec,
            vmem,
            vmem,
            vmem,
            vmem,
            any_spec,
            any_spec,
            any_spec,
            vmem,
            any_spec,
            any_spec,
            vmem,
            vmem,
        ],
        out_specs=(vmem, vmem, vmem),
        scratch_shapes=[
            buf(GROUP, 512),
            buf(512, D),
            buf(D, HIDDEN),
            buf(D, HIDDEN),
            buf(D, HIDDEN),
            buf(D, HIDDEN),
            buf(D, 2 * PAIR_HIDDEN),
            buf(HIDDEN, D),
            buf(4, HIDDEN, D // 2),
            buf(8, 8, 32, QKV),
            buf(8, TOKENS, D),
            buf(8, TOKENS, D),
            buf(4, TOKENS, QUARTER),
            buf(8, TOKENS, QUARTER),
            buf(SLOTS, GROUP),
            buf(GROUP, SLOTS),
            buf(GROUP, SLOTS),
            buf(8, 8, *rows),
            buf(8, 8, *rows),
            buf(4, 8, *rows),
            buf(8, 4, *rows),
            buf(4, 8, *rows),
            buf(8, 4, *rows),
            pltpu.VMEM((ROWS, 2 * PAIR_HIDDEN), F32),
            buf(ROWS, PAIR_HIDDEN),
            buf(ROWS, PAIR_HIDDEN),
            pltpu.VMEM((ROWS, D // 2), F32),
            buf(4, 8, *rows),
            buf(8, 4, *rows),
            buf(8, 8, *rows),
            buf(8, 8, *rows),
            buf(8, TOKENS, QUARTER),
            buf(8, TOKENS, QUARTER),
            buf(TOKENS, D),
            buf(8, TOKENS, D),
            dma((7,)),
            dma((8,)),
            dma((8,)),
            dma((8,)),
            dma((8,)),
            dma((2,)),
            dma((2,)),
            dma((3,)),
            dma((3,)),
            dma((8,)),
            dma((8,)),
            dma((4, 2)),
            dma((4, 2)),
            dma,
            dma,
            dma,
            dma((4,)),
            dma((8,)),
            dma,
            dma((4,)),
            dma((8,)),
            dma,
            dma,
            dma,
            dma,
            dma,
            dma,
            dma((8,)),
            dma((8,)),
            dma((8,)),
            dma((8,)),
        ],
        compiler_params=pltpu.CompilerParams(
            collective_id=0, has_side_effects=True, vmem_limit_bytes=56 * 1024 * 1024
        ),
    )(
        attn_out,
        out_weight,
        residual,
        attn_gain.reshape(1, -1),
        expert_ids,
        route_weights,
        w_gate,
        w_up,
        w_down,
        input_gain.reshape(1, -1),
        q_weight,
        kv_weight,
        q_gain.reshape(1, -1),
        k_gain.reshape(1, -1),
    )


def solution(mesh):
    return jax.shard_map(
        per_device,
        mesh=mesh,
        in_specs=(
            P("expert", "tensor"),
            P("tensor", None),
            P(("expert", "tensor"), None),
            P(),
            P("expert", None),
            P("expert", None),
            P("expert", None, "tensor"),
            P("expert", None, "tensor"),
            P("expert", "tensor", None),
            P(),
            P("expert", "tensor"),
            P("expert", "tensor"),
            P(),
            P(),
        ),
        out_specs=(P(("expert", "tensor"), None), P("expert", "tensor"), P("expert", "tensor")),
        check_vma=False,
    )
```

time: 476 us -> 127 us (0.27)
  the two profiles are of different devices: /device:TPU:1 before, /device:TPU:249 now
where the time goes in v1:
time: 127 us
  Pallas kernels  115 us (91%)
  local copies, waits for them, and re-layouts  10.8 us (9%)
    pallas_call x1, Pallas kernels, per_device(): pl.pallas_call(kernel, out_shape=(jax.ShapeDtypeStruct((TOKENS, D), BF),...  115 us
    unnamed x9, local copies, waits for them, and re-layouts  10.8 us

profile of v1, /device:TPU:249, one launch (start us, length us, event | category | flops | bytes accessed | tf_op | source)
XLA Modules:
  0.0 126.8 jit_solution(11782856352210276677)
XLA Ops:
  0.6 0.0 copy-start
  0.6 1.5 %copy.17.ids_ref = s32[128,8]{1,0:T(8,128)} copy(s32[128,8]{0,1:T(8,128)} %param.18) | data formatting | bytes 8192 | tf_op args[4]
  2.1 1.4 %copy.18.rw_ref = f32[128,8]{1,0:T(8,128)} copy(f32[128,8]{0,1:T(8,128)} %param.19) | data formatting | bytes 8192 | tf_op args[5]
  3.5 2.2 %copy.19.wg_hbm = bf16[1,2048,192]{2,1,0:T(8,128)(2,1)} copy(bf16[1,2048,192]{1,2,0:T(8,128)(2,1)} %param.20) | data formatting | bytes 1572864 | tf_op args[6]
  5.8 0.0 copy-done
  5.8 1.3 %copy.20.wu_hbm = bf16[1,2048,192]{2,1,0:T(8,128)(2,1)} copy(bf16[1,2048,192]{1,2,0:T(8,128)(2,1)S(1)} %copy-done) | data formatting | bytes 1572864 | tf_op args[7]
  7.1 115.3 %shard_map.157 = (bf16[16,2048]{1,0:T(8,128)(2,1)}, bf16[128,512]{1,0:T(8,128)(2,1)}, bf16[128,128]{1,0:T(8,128)(2,1)}) custom-call(bf16[128,512]{1,0:T(8,128)(2,1)} %attn_hbm.1, bf16[512,2048]{1,0:T(8,128)(2,1)} %ow_hbm.1, bf16[16,2048]{1,0:T(8,128)(2,1)} %res_ref.1, f32[1,2048]{1,0:T(1,128)} %bitcast.4, s32[128,8]{1,0:T(8,128)} %copy.17.ids_ref, ...), custom_call_target="tpu_custom_call" | custom-call | tf_op jit(solution)/shard_map/pallas_call | solution.py:628
  122.4 1.5 %copy.24 = bf16[16,2048]{1,0:T(8,128)(2,1)} copy(bf16[16,2048]{1,0:T(8,128)(2,1)} %get-tuple-element.6) | data formatting | bytes 131072
  123.8 1.6 %copy.25 = bf16[128,512]{1,0:T(8,128)(2,1)} copy(bf16[128,512]{1,0:T(8,128)(2,1)} %get-tuple-element.7) | data formatting | bytes 262144
  125.4 1.4 %copy.26 = bf16[128,128]{1,0:T(8,128)(2,1)} copy(bf16[128,128]{1,0:T(8,128)(2,1)} %get-tuple-element.8) | data formatting | bytes 65536
Async XLA Ops:
  0.6 5.1 %copy-start = (bf16[1,2048,192]{1,2,0:T(8,128)(2,1)S(1)}, bf16[1,2048,192]{1,2,0:T(8,128)(2,1)}, u32[]{:S(2)}) copy-start(bf16[1,2048,192]{1,2,0:T(8,128)(2,1)} %param.21) | copy-start | bytes 2359300

commit v2 on v1

v2 whole, which is shorter than its diff:
```python
import jax
import jax.numpy as jnp
from jax import lax
from jax.experimental import pallas as pl
from jax.experimental.pallas import tpu as pltpu
from jax.sharding import PartitionSpec as P

MESH = pl.DeviceIdType.MESH
BF = jnp.bfloat16
F32 = jnp.float32

KV_HEADS = 4
TOP = 8
EPSILON = 1e-06

D = 2048
GROUP = 128
TOKENS = 16
CAP = 12
QUARTER = 512
PIECE = 256
FIRST = 4
HIDDEN = 192
PAIR_HIDDEN = 384
ROWS = 384
SLOTS = 768
QKV = 640
HEAD = 128


def normalize(values, gain):
    return values * lax.rsqrt(jnp.mean(values * values, axis=-1, keepdims=True) + EPSILON) * gain


def dot(a, b):
    return jnp.dot(a, b, preferred_element_type=F32)


def iota(shape, axis):
    return lax.broadcasted_iota(jnp.int32, shape, axis)


def kernel(
    attn_hbm,
    ow_hbm,
    res_ref,
    attn_gain,
    ids_ref,
    rw_ref,
    wg_hbm,
    wu_hbm,
    wd_hbm,
    input_gain,
    qw_hbm,
    kvw_hbm,
    moved_ref,
    raw_ref,
    attn,
    ow,
    gate_up,
    wd_own,
    wd,
    qw,
    partial,
    rs_in,
    normed_out,
    normed_in,
    pick,
    mix_hi,
    mix_lo,
    tx,
    r1,
    x0,
    x1,
    c0,
    c1,
    hidden,
    act,
    act_in,
    y_acc,
    y0,
    y1,
    r3,
    r4,
    sums_out,
    sums_in,
    first,
    nx,
    load_sem,
    rs_send,
    rs_recv,
    nb_send,
    nb_recv,
    pair_send,
    pair_recv,
    wd_send,
    wd_recv,
    q1_send,
    q1_recv,
    q2_send,
    q2_recv,
    d1_send,
    d1_recv,
    d2_send,
    d2_recv0,
    d2_recv1,
    c_send,
    c_recv0,
    c_recv1,
    act_send,
    act_recv,
    r3_send,
    r3_recv,
    r4_send,
    r4_recv,
    sums_send,
    sums_recv,
    nx_send,
    nx_recv,
):
    e = lax.axis_index("expert")
    t = lax.axis_index("tensor")
    z, y = e // 8, e % 8
    core = t % 2
    side = (t // 2) % 2
    parity = t // 4
    partner = t + 1 - 2 * core
    cross = t + 2 - 4 * side
    core0, core1 = t - core, t - core + 1
    half = z // 4
    a = y + core * (z - y)
    b = z + core * (y - z)

    def at(first_axis, second_axis):
        return (second_axis + core * (first_axis - second_axis)) * 8 + (
            first_axis + core * (second_axis - first_axis)
        )

    def step_of(i):
        return jnp.where(i % 2 == 1, (i + 1) // 2, 8 - i // 2)

    def remote(src, dst, send, recv, expert, tensor):
        return pltpu.make_async_remote_copy(
            src_ref=src,
            dst_ref=dst,
            send_sem=send,
            recv_sem=recv,
            device_id={"expert": expert, "tensor": tensor},
            device_id_type=MESH,
        )

    def arrived(dst, send, recv):
        remote(dst, dst, send, recv, e, partner).wait_recv()

    def left(src, send, recv):
        remote(src, src, send, recv, e, partner).wait_send()

    sent, coming = [], {}

    def send(src, dst, send_sem, recv_sem, expert, tensor):
        remote(src, dst, send_sem, recv_sem, expert, tensor).start()
        sent.append(lambda: left(src, send_sem, recv_sem))

    def expect(name, dst, send_sem, recv_sem):
        coming.setdefault(name, []).append(lambda: arrived(dst, send_sem, recv_sem))

    def take(name):
        for wait in coming.pop(name):
            wait()

    def to_tensor(name, src_of, dst, send_sem, recv_sem):
        @pl.loop(1, 8)
        def _(i):
            d = (t + i) % 8
            remote(src_of(d), dst.at[t], send_sem.at[d], recv_sem.at[t], e, d).start()

        def waits():
            @pl.loop(1, 8)
            def _(i):
                s = (t + i) % 8
                arrived(dst.at[s], send_sem.at[s], recv_sem.at[s])

        def gone():
            @pl.loop(1, 8)
            def _(i):
                d = (t + i) % 8
                left(src_of(d), send_sem.at[d], recv_sem.at[d])

        coming[name] = [waits]
        sent.append(gone)

    barrier = pltpu.get_barrier_semaphore()

    @pl.loop(1, 8)
    def _(i):
        pl.semaphore_signal(
            barrier, inc=1, device_id={"expert": e, "tensor": (t + i) % 8}, device_id_type=MESH
        )
        for which in (core0, core1):
            pl.semaphore_signal(
                barrier,
                inc=1,
                device_id={"expert": z * 8 + (y + i) % 8, "tensor": which},
                device_id_type=MESH,
            )
            pl.semaphore_signal(
                barrier,
                inc=1,
                device_id={"expert": ((z + i) % 8) * 8 + y, "tensor": which},
                device_id_type=MESH,
            )

    ow_parts = [
        pltpu.make_async_copy(
            ow_hbm.at[:, pl.ds(n * 512, 512)], ow.at[:, pl.ds(n * 512, 512)], load_sem.at[6 + n]
        )
        for n in range(4)
    ]
    loads = [
        pltpu.make_async_copy(attn_hbm, attn, load_sem.at[0]),
        pltpu.make_async_copy(qw_hbm, qw.at[b, a, :, pl.ds(0, 512)], load_sem.at[1]),
        pltpu.make_async_copy(kvw_hbm, qw.at[b, a, :, pl.ds(512, 128)], load_sem.at[2]),
        pltpu.make_async_copy(wg_hbm.at[0], gate_up.at[0], load_sem.at[3]),
        pltpu.make_async_copy(wu_hbm.at[0], gate_up.at[2], load_sem.at[4]),
        pltpu.make_async_copy(wd_hbm.at[0], wd_own, load_sem.at[5]),
    ]
    loads[0].start()
    for part in ow_parts:
        part.start()
    for load in loads[1:]:
        load.start()

    loads[0].wait()
    for n in range(4):
        ow_parts[n].wait()
        cols = slice(n * 512, n * 512 + 512)
        partial[:, :, cols] = dot(attn[...], ow[:, cols]).astype(BF).reshape(8, TOKENS, 512)

    pl.semaphore_wait(barrier, 35)

    to_tensor("rs", lambda d: partial.at[d], rs_in, rs_send, rs_recv)

    loads[1].wait()
    loads[2].wait()

    @pl.loop(1, 8)
    def _(i):
        d = (a + step_of(i)) % 8
        remote(
            qw.at[b, a], qw.at[b, a], q1_send.at[d], q1_recv.at[a], at(d, b), t
        ).start()

    def q1_left():
        @pl.loop(1, 8)
        def _(i):
            n = (a + i) % 8
            left(qw.at[b, a], q1_send.at[n], q1_recv.at[n])

    sent.append(q1_left)

    loads[3].wait()
    loads[4].wait()
    for k in range(2):
        send(gate_up.at[2 * k], gate_up.at[2 * k + 1], pair_send.at[k], pair_recv.at[k], e, partner)
        expect("pair", gate_up.at[2 * k + 1], pair_send.at[k], pair_recv.at[k])

    position = iota((GROUP, 64), 1)
    p_first, p_second = position // 8, position % 8
    expert_of = 2 * at(p_first, p_second) + parity
    ids = ids_ref[...].T
    weights = rw_ref[...].T
    named = jnp.zeros((GROUP, 64), F32)
    weight_of = jnp.zeros((GROUP, 64), F32)
    for k in range(TOP):
        hit = expert_of == ids[:, k : k + 1]
        named += jnp.where(hit, 1.0, 0.0)
        weight_of += jnp.where(hit, weights[:, k : k + 1], 0.0)
    lower = jnp.where(iota((GROUP, GROUP), 1) < iota((GROUP, GROUP), 0), 1.0, 0.0).astype(BF)
    rank = dot(lower, named.astype(BF))
    code = (named * (rank + 1.0)).astype(BF)
    slot = iota((64, SLOTS), 1)
    start = iota((64, SLOTS), 0) * CAP
    spread = jnp.where((slot >= start) & (slot < start + CAP), 1.0, 0.0).astype(BF)
    wanted = (iota((GROUP, SLOTS), 1) % CAP + 1).astype(F32)
    chosen = dot(code, spread) == wanted
    high = weight_of.astype(BF)
    low = (weight_of - high.astype(F32)).astype(BF)
    mix_hi[...] = jnp.where(chosen, dot(high, spread), 0.0).astype(BF)
    mix_lo[...] = jnp.where(chosen, dot(low, spread), 0.0).astype(BF)
    pick[...] = jnp.where(chosen, 1.0, 0.0).T.astype(BF)

    after, before = at(a, (b + 1) % 8), at(a, (b + 7) % 8)

    def ring(step):
        rows = ((b + 8 - step) % 8, (b + step) % 8)
        if step == 3:
            pieces = (qw.at[rows[0], pl.ds(0, 4)], qw.at[rows[1], pl.ds(4, 4)])
        else:
            pieces = (qw.at[rows[0]], qw.at[rows[1]])
        return [
            remote(pieces[k], pieces[k], q2_send.at[step, k], q2_recv.at[step, k], (after, before)[k], t)
            for k in range(2)
        ]

    def ring_wait(step):
        rows = ((b + 7 - step) % 8, (b + 1 + step) % 8)
        if step == 3:
            pieces = (qw.at[rows[0], pl.ds(0, 4)], qw.at[rows[1], pl.ds(4, 4)])
        else:
            pieces = (qw.at[rows[0]], qw.at[rows[1]])
        for k in range(2):
            arrived(pieces[k], q2_send.at[step, k], q2_recv.at[step, k])

    @pl.loop(1, 8)
    def _(i):
        s = (a + i) % 8
        arrived(qw.at[b, s], q1_send.at[s], q1_recv.at[s])

    def ring_start(step):
        for c in ring(step):
            c.start()
        sent.append(lambda: [c.wait_send() for c in ring(step)])
        coming["ring"] = [lambda: ring_wait(step)]

    ring_start(0)

    rs_in[t] = partial[t]

    take("rs")

    total = res_ref[...].astype(F32)
    attn_sum = rs_in[0].astype(F32)
    for k in range(1, 8):
        attn_sum += rs_in[k].astype(F32)
    first_residual = (total + attn_sum).astype(BF)
    first[...] = first_residual
    normed = normalize(first_residual.astype(F32), attn_gain[...]).astype(BF)
    for s in range(4):
        normed_out[s] = normed[:, s * QUARTER : s * QUARTER + QUARTER]
    normed_in[t] = normed_out[t % 4]

    to_tensor("nb", lambda d: normed_out.at[d % 4], normed_in, nb_send, nb_recv)

    loads[5].wait()
    own_half = pl.ds(pl.multiple_of(side * 1024, 1024), 1024)
    other_half = pl.ds(pl.multiple_of((1 - side) * 1024, 1024), 1024)
    send(wd_own.at[:, own_half], wd.at[1], wd_send.at[0], wd_recv.at[0], e, partner)
    expect("wd", wd.at[1], wd_send.at[0], wd_recv.at[0])
    send(wd_own.at[:, other_half], wd.at[2], wd_send.at[1], wd_recv.at[1], e, cross)
    expect("wd cross", wd.at[2], wd_send.at[1], wd_recv.at[1])
    wd[0] = wd_own[:, own_half]

    take("nb")

    group = normed_in[...].reshape(GROUP, QUARTER)

    def gone_d2():
        @pl.when(core == 0)
        def _():
            left(r1.at[0, pl.ds(0, 7)], d2_send, d2_recv0.at[0, 0])

            @pl.when(half == 1)
            def _():
                left(r1.at[0, 0], d2_send, d2_recv0.at[0, 0])

        @pl.when(core == 1)
        def _():
            left(r1.at[0, pl.ds(0, 7)], d2_send, d2_recv0.at[0, 0])
            left(r1.at[0, 0, pl.ds(0, 4)], d2_send, d2_recv0.at[0, 0])

    def dispatch_first(p):
        for k in range(2):
            rows = slice(k * 384, k * 384 + 384)
            tx[p, 4 * k : 4 * k + 4] = (
                dot(pick[rows, :], group[:, p * PIECE : p * PIECE + PIECE])
                .astype(BF)
                .reshape(4, 8, 3, 4, PIECE)
            )

        @pl.loop(1, 8)
        def _(i):
            d = (a + step_of(i)) % 8
            remote(tx.at[p, d], r1.at[p, a], d1_send, d1_recv.at[p], at(d, b), t).start()

        pltpu.make_async_copy(tx.at[p, a], r1.at[p, a], d1_recv.at[p]).start()
        sent.append(lambda: left(tx.at[p, pl.ds(0, 7)], d1_send, d1_recv.at[p]))

    def dispatch_second(p):
        arrived(r1.at[p], d1_send, d1_recv.at[p])

        def core0_path(d):
            return r1.at[p, :, d], x0.at[p, z % 4], d2_recv0.at[p, z % 4]

        def core1_path(d, hf):
            return r1.at[p, pl.ds(4 * hf, 4), d], x1.at[p, y], d2_recv1.at[p, y]

        @pl.when(core == 0)
        def _():
            src, dst, sem = core0_path(b)

            @pl.when(half == 0)
            def _():
                pltpu.make_async_copy(src, dst, sem).start()

            @pl.when(half == 1)
            def _():
                remote(src, dst, d2_send, sem, e, core1).start()

            @pl.loop(1, 8)
            def _(i):
                d = (b + step_of(i)) % 8
                src, dst, sem = core0_path(d)
                remote(src, dst, d2_send, sem, at(a, d), core0 + half).start()

        @pl.when(core == 1)
        def _():
            src, dst, sem = core1_path(b, 0)
            remote(src, dst, d2_send, sem, e, core0).start()
            src, dst, sem = core1_path(b, 1)
            pltpu.make_async_copy(src, dst, sem).start()

            @pl.loop(1, 8)
            def _(i):
                d = (b + step_of(i)) % 8
                for hf in range(2):
                    src, dst, sem = core1_path(d, hf)
                    remote(src, dst, d2_send, sem, at(a, d), core0 + hf).start()

        sent.append(gone_d2)

    def forward0(p, k):
        arrived(x0.at[p, k], c_send, d2_recv0.at[p, k])
        remote(x0.at[p, k], c0.at[p, k], c_send, c_recv0.at[p, k], e, cross).start()

    def forward1(p, i):
        k = (y + step_of(i)) % 8
        arrived(x1.at[p, k], c_send, d2_recv1.at[p, k])
        remote(x1.at[p, k], c1.at[p, k], c_send, c_recv1.at[p, k], e, cross).start()

    def forward_rest(p):
        @pl.loop(0, 4)
        def _(i):
            forward0(p, i)

            @pl.when(i >= FIRST // 2)
            def _():
                forward1(p, 2 * i)
                forward1(p, 2 * i + 1)

        sent.append(lambda: (left(x0.at[p], c_send, c_recv0.at[p, 0]), left(x1.at[p], c_send, c_recv0.at[p, 0])))

    def forward_first(p):
        @pl.loop(0, FIRST)
        def _(i):
            forward1(p, i)

    def take_c0(p):
        @pl.loop(0, 4)
        def _(i):
            arrived(c0.at[p, i], c_send, c_recv0.at[p, i])

    def take_c1(p):
        @pl.loop(0, 8)
        def _(i):
            arrived(c1.at[p, i], c_send, c_recv1.at[p, i])

    def multiply(values, column, zero=False):
        rows = pl.ds(pl.multiple_of(column, PIECE), PIECE)
        for n in range(2):
            cols = slice(n * PAIR_HIDDEN, n * PAIR_HIDDEN + PAIR_HIDDEN)
            product = lax.dot_general(
                values,
                gate_up[2 * n : 2 * n + 2, :, rows].reshape(PAIR_HIDDEN, PIECE),
                (((1,), (1,)), ((), ())),
                preferred_element_type=F32,
            )
            hidden[:, cols] = product if zero else hidden[:, cols] + product

    def natural(ref, p):
        return ref[p].reshape(ROWS, PIECE)

    def turned(ref, p):
        return jnp.concatenate([ref[p, :, k].reshape(96, PIECE) for k in range(4)], axis=0)

    own, other = side * 1024, (1 - side) * 1024

    dispatch_first(0)
    dispatch_first(1)
    take("pair")
    take("wd cross")
    send(wd.at[2], wd.at[3], wd_send.at[2], wd_recv.at[2], e, partner)
    expect("wd", wd.at[3], wd_send.at[2], wd_recv.at[2])
    dispatch_second(0)
    forward_first(0)
    dispatch_second(1)
    forward_rest(0)
    multiply(natural(x0, 0), own, True)
    multiply(turned(x1, 0), own + QUARTER)
    forward_first(1)
    forward_rest(1)
    take("ring")
    ring_start(1)
    multiply(natural(x0, 1), own + PIECE)
    multiply(turned(x1, 1), own + QUARTER + PIECE)
    take_c0(0)
    multiply(natural(c0, 0), other)
    take_c1(0)
    multiply(turned(c1, 0), other + QUARTER)
    take("ring")
    ring_start(2)
    take_c0(1)
    multiply(natural(c0, 1), other + PIECE)
    take_c1(1)
    multiply(turned(c1, 1), other + QUARTER + PIECE)

    gate = hidden[:, 0:PAIR_HIDDEN]
    act[...] = (
        gate * (1.0 / (1.0 + jnp.exp(-gate))) * hidden[:, PAIR_HIDDEN : 2 * PAIR_HIDDEN]
    ).astype(BF)
    send(act, act_in, act_send, act_recv, e, cross)

    take("wd")
    for n in range(4):
        cols = slice(n * 256, n * 256 + 256)
        y_acc[:, cols] = dot(act[...], wd[0:2, :, cols].reshape(PAIR_HIDDEN, 256))
    take("ring")
    ring_start(3)
    arrived(act_in, act_send, act_recv)

    first_zone = 4 * core

    def gone_r3():
        left(y1.at[0, pl.ds(0, 7)], r3_send, r3_recv.at[0])

        @pl.when((core == 0) & (half == 0))
        def _():
            left(y0.at[0, pl.ds(0, 3)], r3_send, r3_recv.at[0])
            left(y1.at[0, 0], r3_send, r3_recv.at[0])

        @pl.when((core == 0) & (half == 1))
        def _():
            left(y0.at[0], r3_send, r3_recv.at[0])
            left(y1.at[0, 0], r3_send, r3_recv.at[0])

        @pl.when(core == 1)
        def _():
            left(y0.at[0], r3_send, r3_recv.at[0])

    for p in range(2):
        for n in (p, 2 + p):
            cols = slice(n * PIECE, n * PIECE + PIECE)
            out = y_acc[:, cols] + dot(act_in[...], wd[2:4, :, cols].reshape(PAIR_HIDDEN, PIECE))
            blocks = out.astype(BF).reshape(4, 8, 3, 4, PIECE)
            if n < 2:
                y0[p] = blocks
            else:
                for k in range(4):
                    y1[p, :, k] = blocks[k]

        @pl.loop(0, 4)
        def _(i):
            zone = first_zone + i
            src, dst = y0.at[p, i], r3.at[p, z]

            @pl.when(zone != z)
            def _():
                remote(src, dst, r3_send, r3_recv.at[p], zone * 8 + y, core0).start()

            @pl.when((zone == z) & (core == 0))
            def _():
                pltpu.make_async_copy(src, dst, r3_recv.at[p]).start()

            @pl.when((zone == z) & (core == 1))
            def _():
                remote(src, dst, r3_send, r3_recv.at[p], e, core0).start()

        into = r3.at[p, y, pl.ds(first_zone, 4)]

        @pl.loop(1, 8)
        def _(i):
            d = (y + step_of(i)) % 8
            remote(y1.at[p, d], into, r3_send, r3_recv.at[p], z * 8 + d, core1).start()

        @pl.when(core == 1)
        def _():
            pltpu.make_async_copy(y1.at[p, y], into, r3_recv.at[p]).start()

        @pl.when(core == 0)
        def _():
            remote(y1.at[p, y], into, r3_send, r3_recv.at[p], e, core1).start()

        sent.append(gone_r3)

    for p in range(2):
        arrived(r3.at[p], r3_send, r3_recv.at[p])

        @pl.loop(1, 8)
        def _(i):
            d = (a + step_of(i)) % 8
            remote(r3.at[p, :, d], r4.at[p, a], r4_send, r4_recv.at[p], at(d, b), t).start()

        pltpu.make_async_copy(r3.at[p, :, a], r4.at[p, a], r4_recv.at[p]).start()
        sent.append(lambda: left(r4.at[0, pl.ds(0, 7)], r4_send, r4_recv.at[0]))

    for p in range(2):
        arrived(r4.at[p], r4_send, r4_recv.at[p])
        returned = r4[p].reshape(SLOTS, PIECE)
        weighted = dot(mix_hi[...], returned) + dot(mix_lo[...], returned)
        sums_out[:, :, p * PIECE : p * PIECE + PIECE] = weighted.astype(BF).reshape(
            8, TOKENS, PIECE
        )
    sums_in[t] = sums_out[t]

    to_tensor("sums", lambda d: sums_out.at[d], sums_in, sums_send, sums_recv)
    take("sums")

    expert_sum = jnp.concatenate(
        [sums_in[s].astype(F32) + sums_in[s + 4].astype(F32) for s in range(4)], axis=1
    )
    next_residual = (first[...].astype(F32) + expert_sum).astype(BF)
    moved_ref[...] = next_residual
    nx[t] = normalize(next_residual.astype(F32), input_gain[...]).astype(BF)

    to_tensor("nx", lambda d: nx.at[t], nx, nx_send, nx_recv)

    take("ring")

    take("nx")

    tokens = nx[...].reshape(GROUP, D)
    raw = jnp.zeros((GROUP, QKV), F32)
    for zz in range(8):
        blocks = []
        for yy in range(8):
            second = zz + core * (yy - zz)
            blocks.append(qw[second, yy + core * (zz - yy)])
        raw += dot(tokens[:, zz * 256 : zz * 256 + 256], jnp.concatenate(blocks, axis=0))
    raw_ref[...] = raw

    for gone in sent:
        gone()


def finish(moved_ref, raw_ref, q_gain, k_gain, next_ref, queries_ref, kv_ref):
    t = lax.axis_index("tensor")
    next_ref[...] = moved_ref[...]
    for head in range(4):
        cols = slice(head * HEAD, head * HEAD + HEAD)
        queries_ref[:, cols] = normalize(raw_ref[:, cols], q_gain[...]).astype(BF)
    kv_raw = raw_ref[:, 512:QKV]
    kv_ref[...] = jnp.where(t < KV_HEADS, normalize(kv_raw, k_gain[...]), kv_raw).astype(BF)


def per_device(
    attn_out,
    out_weight,
    residual,
    attn_gain,
    expert_ids,
    route_weights,
    w_gate,
    w_up,
    w_down,
    input_gain,
    q_weight,
    kv_weight,
    q_gain,
    k_gain,
):
    any_spec = pl.BlockSpec(memory_space=pl.ANY)
    vmem = pl.BlockSpec(memory_space=pltpu.VMEM)
    dma = pltpu.SemaphoreType.DMA
    rows = (3, 4, PIECE)

    def buf(*shape):
        return pltpu.VMEM(shape, BF)

    moved, raw = pl.pallas_call(
        kernel,
        out_shape=(
            jax.ShapeDtypeStruct((TOKENS, D), BF),
            jax.ShapeDtypeStruct((GROUP, QKV), F32),
        ),
        in_specs=[
            any_spec,
            any_spec,
            vmem,
            vmem,
            vmem,
            vmem,
            any_spec,
            any_spec,
            any_spec,
            vmem,
            any_spec,
            any_spec,
        ],
        out_specs=(vmem, vmem),
        scratch_shapes=[
            buf(GROUP, 512),
            buf(512, D),
            buf(4, HIDDEN, D),
            buf(HIDDEN, D),
            buf(4, HIDDEN, D // 2),
            buf(8, 8, 32, QKV),
            buf(8, TOKENS, D),
            buf(8, TOKENS, D),
            buf(4, TOKENS, QUARTER),
            buf(8, TOKENS, QUARTER),
            buf(SLOTS, GROUP),
            buf(GROUP, SLOTS),
            buf(GROUP, SLOTS),
            buf(2, 8, 8, *rows),
            buf(2, 8, 8, *rows),
            buf(2, 4, 8, *rows),
            buf(2, 8, 4, *rows),
            buf(2, 4, 8, *rows),
            buf(2, 8, 4, *rows),
            pltpu.VMEM((ROWS, 2 * PAIR_HIDDEN), F32),
            buf(ROWS, PAIR_HIDDEN),
            buf(ROWS, PAIR_HIDDEN),
            pltpu.VMEM((ROWS, D // 2), F32),
            buf(2, 4, 8, *rows),
            buf(2, 8, 4, *rows),
            buf(2, 8, 8, *rows),
            buf(2, 8, 8, *rows),
            buf(8, TOKENS, QUARTER),
            buf(8, TOKENS, QUARTER),
            buf(TOKENS, D),
            buf(8, TOKENS, D),
            dma((10,)),
            dma((8,)),
            dma((8,)),
            dma((8,)),
            dma((8,)),
            dma((2,)),
            dma((2,)),
            dma((3,)),
            dma((3,)),
            dma((8,)),
            dma((8,)),
            dma((4, 2)),
            dma((4, 2)),
            dma,
            dma((2,)),
            dma,
            dma((2, 4)),
            dma((2, 8)),
            dma,
            dma((2, 4)),
            dma((2, 8)),
            dma,
            dma,
            dma,
            dma((2,)),
            dma,
            dma((2,)),
            dma((8,)),
            dma((8,)),
            dma((8,)),
            dma((8,)),
        ],
        compiler_params=pltpu.CompilerParams(
            collective_id=0, has_side_effects=True, vmem_limit_bytes=66_400_000
        ),
    )(
        attn_out,
        out_weight,
        residual,
        attn_gain.reshape(1, -1),
        expert_ids.T,
        route_weights.T,
        jnp.swapaxes(w_gate, 1, 2),
        jnp.swapaxes(w_up, 1, 2),
        w_down,
        input_gain.reshape(1, -1),
        q_weight,
        kv_weight,
    )
    return pl.pallas_call(
        finish,
        out_shape=(
            jax.ShapeDtypeStruct((TOKENS, D), BF),
            jax.ShapeDtypeStruct((GROUP, 512), BF),
            jax.ShapeDtypeStruct((GROUP, HEAD), BF),
        ),
        in_specs=[vmem] * 4,
        out_specs=(vmem, vmem, vmem),
        compiler_params=pltpu.CompilerParams(vmem_limit_bytes=4 * 1024 * 1024),
    )(moved, raw, q_gain.reshape(1, -1), k_gain.reshape(1, -1))


def solution(mesh):
    return jax.shard_map(
        per_device,
        mesh=mesh,
        in_specs=(
            P("expert", "tensor"),
            P("tensor", None),
            P(("expert", "tensor"), None),
            P(),
            P("expert", None),
            P("expert", None),
            P("expert", None, "tensor"),
            P("expert", None, "tensor"),
            P("expert", "tensor", None),
            P(),
            P("expert", "tensor"),
            P("expert", "tensor"),
            P(),
            P(),
        ),
        out_specs=(P(("expert", "tensor"), None), P("expert", "tensor"), P("expert", "tensor")),
        check_vma=False,
    )
```

time: 127 us -> 111 us (0.87)
  the two profiles are of different devices: /device:TPU:249 before, /device:TPU:1 now
where the time goes in v2:
time: 111 us
  Pallas kernels  108 us (97%)
  local copies, waits for them, and re-layouts  1.81 us (2%)
    pallas_call x1, Pallas kernels, per_device(): pl.pallas_call(kernel, out_shape=(jax.ShapeDtypeStruct((TOKENS, D), BF),...  108 us

profile of v2, /device:TPU:1, one launch (start us, length us, event | category | flops | bytes accessed | tf_op | source)
XLA Modules:
  0.0 110.9 jit_solution(13266121488559304376)
XLA Ops:
  0.6 0.0 copy-start.2
  0.6 0.0 copy-start.3
  0.7 107.6 %shard_map.157 = (bf16[16,2048]{1,0:T(8,128)(2,1)}, f32[128,640]{1,0:T(8,128)}) custom-call(bf16[128,512]{1,0:T(8,128)(2,1)} %attn_hbm.1, bf16[512,2048]{1,0:T(8,128)(2,1)} %ow_hbm.1, bf16[16,2048]{1,0:T(8,128)(2,1)} %res_ref.1, f32[1,2048]{1,0:T(1,128)} %bitcast.12, s32[8,128]{1,0:T(8,128)} %bitcast.14, f32[8,128]{1,0:T(8,128)} %bitcast.15, ...), custom_call_target="tpu_custom_call" | custom-call | tf_op jit(solution)/shard_map/pallas_call | solution.py:678
  108.2 0.0 copy-done.2
  108.2 0.0 copy-done.3
  108.2 0.0 copy-start
  108.2 1.0 copy-done
  109.2 0.0 copy-start.1
  109.2 0.8 copy-done.1
  110.1 0.8 shard_map.158
Async XLA Ops:
  0.6 107.6 %copy-start.2 = (f32[128]{0:T(128)S(1)}, f32[128]{0:T(128)}, u32[]{:S(2)}) copy-start(f32[128]{0:T(128)} %param.26) | copy-start | bytes 1540
  0.6 107.6 %copy-start.3 = (f32[128]{0:T(128)S(1)}, f32[128]{0:T(128)}, u32[]{:S(2)}) copy-start(f32[128]{0:T(128)} %param.27) | copy-start | bytes 1540
  108.2 1.0 copy-start
  109.2 0.8 copy-start.1

commit v3 on v2

--- a/solution.py
+++ b/solution.py
@@ -62,6 +62,8 @@
     wd,
     qw,
     partial,
+    mates,
+    sums_of_chip,
     rs_in,
     normed_out,
     normed_in,
@@ -87,6 +89,8 @@
     first,
     nx,
     load_sem,
+    mate_send,
+    mate_recv,
     rs_send,
     rs_recv,
     nb_send,
@@ -124,6 +128,7 @@
     core = t % 2
     side = (t // 2) % 2
     parity = t // 4
+    chip = t // 2
     partner = t + 1 - 2 * core
     cross = t + 2 - 4 * side
     core0, core1 = t - core, t - core + 1
@@ -238,7 +243,20 @@
 
     pl.semaphore_wait(barrier, 35)
 
-    to_tensor("rs", lambda d: partial.at[d], rs_in, rs_send, rs_recv)
+    for k in range(4):
+        theirs = 2 * k + 1 - core
+        send(partial.at[theirs], mates.at[k], mate_send.at[k], mate_recv.at[k], e, partner)
+
+    def chip_sum(k):
+        arrived(mates.at[k], mate_send.at[k], mate_recv.at[k])
+        return (partial[2 * k + core].astype(F32) + mates[k].astype(F32)).astype(BF)
+
+    for i in (2, 1, 3):
+        k = (chip + i) % 4
+        sums_of_chip[k] = chip_sum(k)
+        send(sums_of_chip.at[k], rs_in.at[chip], rs_send.at[k], rs_recv.at[chip], e, 2 * k + core)
+        expect("rs", rs_in.at[k], rs_send.at[k], rs_recv.at[k])
+    rs_in[chip] = chip_sum(chip)
 
     loads[1].wait()
     loads[2].wait()
@@ -324,13 +342,11 @@
 
     ring_start(0)
 
-    rs_in[t] = partial[t]
-
     take("rs")
 
     total = res_ref[...].astype(F32)
     attn_sum = rs_in[0].astype(F32)
-    for k in range(1, 8):
+    for k in range(1, 4):
         attn_sum += rs_in[k].astype(F32)
     first_residual = (total + attn_sum).astype(BF)
     first[...] = first_residual
@@ -506,8 +522,6 @@
     multiply(natural(c0, 0), other)
     take_c1(0)
     multiply(turned(c1, 0), other + QUARTER)
-    take("ring")
-    ring_start(2)
     take_c0(1)
     multiply(natural(c0, 1), other + PIECE)
     take_c1(1)
@@ -518,13 +532,13 @@
         gate * (1.0 / (1.0 + jnp.exp(-gate))) * hidden[:, PAIR_HIDDEN : 2 * PAIR_HIDDEN]
     ).astype(BF)
     send(act, act_in, act_send, act_recv, e, cross)
+    take("ring")
+    ring_start(2)
 
     take("wd")
     for n in range(4):
         cols = slice(n * 256, n * 256 + 256)
         y_acc[:, cols] = dot(act[...], wd[0:2, :, cols].reshape(PAIR_HIDDEN, 256))
-    take("ring")
-    ring_start(3)
     arrived(act_in, act_send, act_recv)
 
     first_zone = 4 * core
@@ -612,6 +626,8 @@
     sums_in[t] = sums_out[t]
 
     to_tensor("sums", lambda d: sums_out.at[d], sums_in, sums_send, sums_recv)
+    take("ring")
+    ring_start(3)
     take("sums")
 
     expert_sum = jnp.concatenate(
@@ -621,11 +637,20 @@
     moved_ref[...] = next_residual
     nx[t] = normalize(next_residual.astype(F32), input_gain[...]).astype(BF)
 
-    to_tensor("nx", lambda d: nx.at[t], nx, nx_send, nx_recv)
+    for i in (2, 1, 3):
+        d = 2 * ((chip + i) % 4) + core
+        send(nx.at[t], nx.at[t], nx_send.at[i], nx_recv.at[t], e, d)
+    send(nx.at[t], nx.at[t], nx_send.at[0], nx_recv.at[t], e, partner)
+    for i in (1, 3, 2):
+        s = 2 * ((chip + i) % 4) + core
+        arrived(nx.at[s], nx_send.at[i], nx_recv.at[s])
+        send(nx.at[s], nx.at[s], nx_send.at[4 + i], nx_recv.at[s], e, partner)
 
     take("ring")
 
-    take("nx")
+    for i in range(4):
+        s = 2 * ((chip + i) % 4) + 1 - core
+        arrived(nx.at[s], nx_send.at[i], nx_recv.at[s])
 
     tokens = nx[...].reshape(GROUP, D)
     raw = jnp.zeros((GROUP, QKV), F32)
@@ -704,7 +729,9 @@
             buf(4, HIDDEN, D // 2),
             buf(8, 8, 32, QKV),
             buf(8, TOKENS, D),
-            buf(8, TOKENS, D),
+            buf(4, TOKENS, D),
+            buf(4, TOKENS, D),
+            buf(4, TOKENS, D),
             buf(4, TOKENS, QUARTER),
             buf(8, TOKENS, QUARTER),
             buf(SLOTS, GROUP),
@@ -729,8 +756,10 @@
             buf(TOKENS, D),
             buf(8, TOKENS, D),
             dma((10,)),
-            dma((8,)),
-            dma((8,)),
+            dma((4,)),
+            dma((4,)),
+            dma((4,)),
+            dma((4,)),
             dma((8,)),
             dma((8,)),
             dma((2,)),
@@ -786,7 +815,7 @@
         ),
         in_specs=[vmem] * 4,
         out_specs=(vmem, vmem, vmem),
-        compiler_params=pltpu.CompilerParams(vmem_limit_bytes=4 * 1024 * 1024),
+        compiler_params=pltpu.CompilerParams(vmem_limit_bytes=66_400_000),
     )(moved, raw, q_gain.reshape(1, -1), k_gain.reshape(1, -1))
 
 

time: 111 us -> 107 us (0.964)
  Pallas kernels: 108 us -> 106 us
  local copies, waits for them, and re-layouts: 1.81 us -> 0 us
    pallas_call x1, Pallas kernels: 108 us -> 104 us  [per_device(): pl.pallas_call(kernel, out_shape=(jax.ShapeDtypeStruct((TOKENS, D), BF),...]
    unnamed x8 -> x0, local copies, waits for them, and re-layouts: 1.81 us -> none
where the time goes in v3:
time: 107 us
  Pallas kernels  106 us (99%)
    pallas_call x1, Pallas kernels, per_device(): pl.pallas_call(kernel, out_shape=(jax.ShapeDtypeStruct((TOKENS, D), BF),...  104 us

profile of v3, /device:TPU:1, one launch (start us, length us, event | category | flops | bytes accessed | tf_op | source)
XLA Modules:
  0.0 106.7 jit_solution(5458529877230551441)
XLA Ops:
  0.6 104.3 %shard_map.157 = (bf16[16,2048]{1,0:T(8,128)(2,1)}, f32[128,640]{1,0:T(8,128)}) custom-call(bf16[128,512]{1,0:T(8,128)(2,1)} %attn_hbm.1, bf16[512,2048]{1,0:T(8,128)(2,1)} %ow_hbm.1, bf16[16,2048]{1,0:T(8,128)(2,1)} %res_ref.1, f32[1,2048]{1,0:T(1,128)} %bitcast.10, s32[8,128]{1,0:T(8,128)} %bitcast.12, f32[8,128]{1,0:T(8,128)} %bitcast.13, ...), custom_call_target="tpu_custom_call" | custom-call | tf_op jit(solution)/shard_map/pallas_call | solution.py:703
  104.9 1.8 %shard_map.158 = (bf16[16,2048]{1,0:T(8,128)(2,1)}, bf16[128,512]{1,0:T(8,128)(2,1)}, bf16[128,128]{1,0:T(8,128)(2,1)}) custom-call(bf16[16,2048]{1,0:T(8,128)(2,1)} %get-tuple-element.5.moved_ref, f32[128,640]{1,0:T(8,128)} %get-tuple-element.6.raw_ref, f32[1,128]{1,0:T(1,128)} %bitcast.14, f32[1,128]{1,0:T(1,128)} %bitcast.15), custom_call_target="tpu_custom_call" | custom-call | tf_op jit(solution)/shard_map/pallas_call | solution.py:809

commit v4 on v3

--- a/solution.py
+++ b/solution.py
@@ -144,6 +144,9 @@
     def step_of(i):
         return jnp.where(i % 2 == 1, (i + 1) // 2, 8 - i // 2)
 
+    def far_first(i):
+        return jnp.where(i % 2 == 1, 4 + (i - 1) // 2, 4 - i // 2)
+
     def remote(src, dst, send, recv, expert, tensor):
         return pltpu.make_async_remote_copy(
             src_ref=src,
@@ -395,7 +398,7 @@
 
         @pl.loop(1, 8)
         def _(i):
-            d = (a + step_of(i)) % 8
+            d = (a + far_first(i)) % 8
             remote(tx.at[p, d], r1.at[p, a], d1_send, d1_recv.at[p], at(d, b), t).start()
 
         pltpu.make_async_copy(tx.at[p, a], r1.at[p, a], d1_recv.at[p]).start()
@@ -592,7 +595,7 @@
 
         @pl.loop(1, 8)
         def _(i):
-            d = (y + step_of(i)) % 8
+            d = (y + far_first(i)) % 8
             remote(y1.at[p, d], into, r3_send, r3_recv.at[p], z * 8 + d, core1).start()
 
         @pl.when(core == 1)
@@ -610,7 +613,7 @@
 
         @pl.loop(1, 8)
         def _(i):
-            d = (a + step_of(i)) % 8
+            d = (a + far_first(i)) % 8
             remote(r3.at[p, :, d], r4.at[p, a], r4_send, r4_recv.at[p], at(d, b), t).start()
 
         pltpu.make_async_copy(r3.at[p, :, a], r4.at[p, a], r4_recv.at[p]).start()

time: 107 us -> 109 us (1.019)
  the two profiles are of different devices: /device:TPU:1 before, /device:TPU:153 now
where the time goes in v4:
time: 109 us
  Pallas kernels  108 us (99%)
    pallas_call x1, Pallas kernels, per_device(): pl.pallas_call(kernel, out_shape=(jax.ShapeDtypeStruct((TOKENS, D), BF),...  106 us

profile of v4, /device:TPU:153, one launch (start us, length us, event | category | flops | bytes accessed | tf_op | source)
XLA Modules:
  0.0 108.7 jit_solution(15157682145156665397)
XLA Ops:
  0.6 106.2 %shard_map.157 = (bf16[16,2048]{1,0:T(8,128)(2,1)}, f32[128,640]{1,0:T(8,128)}) custom-call(bf16[128,512]{1,0:T(8,128)(2,1)} %attn_hbm.1, bf16[512,2048]{1,0:T(8,128)(2,1)} %ow_hbm.1, bf16[16,2048]{1,0:T(8,128)(2,1)} %res_ref.1, f32[1,2048]{1,0:T(1,128)} %bitcast.10, s32[8,128]{1,0:T(8,128)} %bitcast.12, f32[8,128]{1,0:T(8,128)} %bitcast.13, ...), custom_call_target="tpu_custom_call" | custom-call | tf_op jit(solution)/shard_map/pallas_call | solution.py:706
  106.9 1.8 %shard_map.158 = (bf16[16,2048]{1,0:T(8,128)(2,1)}, bf16[128,512]{1,0:T(8,128)(2,1)}, bf16[128,128]{1,0:T(8,128)(2,1)}) custom-call(bf16[16,2048]{1,0:T(8,128)(2,1)} %get-tuple-element.5.moved_ref, f32[128,640]{1,0:T(8,128)} %get-tuple-element.6.raw_ref, f32[1,128]{1,0:T(1,128)} %bitcast.14, f32[1,128]{1,0:T(1,128)} %bitcast.15), custom_call_target="tpu_custom_call" | custom-call | tf_op jit(solution)/shard_map/pallas_call | solution.py:812

commit v5 on v3

--- a/solution.py
+++ b/solution.py
@@ -527,11 +527,14 @@
     take_c1(1)
     multiply(turned(c1, 1), other + QUARTER + PIECE)
 
-    gate = hidden[:, 0:PAIR_HIDDEN]
-    act[...] = (
-        gate * (1.0 / (1.0 + jnp.exp(-gate))) * hidden[:, PAIR_HIDDEN : 2 * PAIR_HIDDEN]
-    ).astype(BF)
-    send(act, act_in, act_send, act_recv, e, cross)
+    for r in range(2):
+        rows = slice(r * 192, r * 192 + 192)
+        gate = hidden[rows, 0:PAIR_HIDDEN]
+        act[rows, :] = (
+            gate * (1.0 / (1.0 + jnp.exp(-gate))) * hidden[rows, PAIR_HIDDEN : 2 * PAIR_HIDDEN]
+        ).astype(BF)
+        part = pl.ds(r * 192, 192)
+        send(act.at[part], act_in.at[part], act_send.at[r], act_recv.at[r], e, cross)
     take("ring")
     ring_start(2)
 
@@ -539,7 +542,6 @@
     for n in range(4):
         cols = slice(n * 256, n * 256 + 256)
         y_acc[:, cols] = dot(act[...], wd[0:2, :, cols].reshape(PAIR_HIDDEN, 256))
-    arrived(act_in, act_send, act_recv)
 
     first_zone = 4 * core
 
@@ -560,49 +562,59 @@
         def _():
             left(y0.at[0], r3_send, r3_recv.at[0])
 
+    for r in range(2):
+        rows = slice(r * 192, r * 192 + 192)
+        zones = slice(2 * r, 2 * r + 2)
+        arrived(act_in.at[pl.ds(r * 192, 192)], act_send.at[r], act_recv.at[r])
+        for p in range(2):
+            for n in (p, 2 + p):
+                cols = slice(n * PIECE, n * PIECE + PIECE)
+                out = y_acc[rows, cols] + dot(
+                    act_in[rows, :], wd[2:4, :, cols].reshape(PAIR_HIDDEN, PIECE)
+                )
+                blocks = out.astype(BF).reshape(2, 8, 3, 4, PIECE)
+                if n < 2:
+                    y0[p, zones] = blocks
+                else:
+                    for k in range(2):
+                        y1[p, :, 2 * r + k] = blocks[k]
+
+            @pl.loop(2 * r, 2 * r + 2)
+            def _(i):
+                zone = first_zone + i
+                src, dst = y0.at[p, i], r3.at[p, z]
+
+                @pl.when(zone != z)
+                def _():
+                    remote(src, dst, r3_send, r3_recv.at[p], zone * 8 + y, core0).start()
+
+                @pl.when((zone == z) & (core == 0))
+                def _():
+                    pltpu.make_async_copy(src, dst, r3_recv.at[p]).start()
+
+                @pl.when((zone == z) & (core == 1))
+                def _():
+                    remote(src, dst, r3_send, r3_recv.at[p], e, core0).start()
+
+            into = r3.at[p, y, pl.ds(first_zone + 2 * r, 2)]
+            part = pl.ds(2 * r, 2)
+
+            @pl.loop(1, 8)
+            def _(i):
+                d = (y + step_of(i)) % 8
+                remote(
+                    y1.at[p, d, part], into, r3_send, r3_recv.at[p], z * 8 + d, core1
+                ).start()
+
+            @pl.when(core == 1)
+            def _():
+                pltpu.make_async_copy(y1.at[p, y, part], into, r3_recv.at[p]).start()
+
+            @pl.when(core == 0)
+            def _():
+                remote(y1.at[p, y, part], into, r3_send, r3_recv.at[p], e, core1).start()
+
     for p in range(2):
-        for n in (p, 2 + p):
-            cols = slice(n * PIECE, n * PIECE + PIECE)
-            out = y_acc[:, cols] + dot(act_in[...], wd[2:4, :, cols].reshape(PAIR_HIDDEN, PIECE))
-            blocks = out.astype(BF).reshape(4, 8, 3, 4, PIECE)
-            if n < 2:
-                y0[p] = blocks
-            else:
-                for k in range(4):
-                    y1[p, :, k] = blocks[k]
-
-        @pl.loop(0, 4)
-        def _(i):
-            zone = first_zone + i
-            src, dst = y0.at[p, i], r3.at[p, z]
-
-            @pl.when(zone != z)
-            def _():
-                remote(src, dst, r3_send, r3_recv.at[p], zone * 8 + y, core0).start()
-
-            @pl.when((zone == z) & (core == 0))
-            def _():
-                pltpu.make_async_copy(src, dst, r3_recv.at[p]).start()
-
-            @pl.when((zone == z) & (core == 1))
-            def _():
-                remote(src, dst, r3_send, r3_recv.at[p], e, core0).start()
-
-        into = r3.at[p, y, pl.ds(first_zone, 4)]
-
-        @pl.loop(1, 8)
-        def _(i):
-            d = (y + step_of(i)) % 8
-            remote(y1.at[p, d], into, r3_send, r3_recv.at[p], z * 8 + d, core1).start()
-
-        @pl.when(core == 1)
-        def _():
-            pltpu.make_async_copy(y1.at[p, y], into, r3_recv.at[p]).start()
-
-        @pl.when(core == 0)
-        def _():
-            remote(y1.at[p, y], into, r3_send, r3_recv.at[p], e, core1).start()
-
         sent.append(gone_r3)
 
     for p in range(2):
@@ -778,8 +790,8 @@
             dma,
             dma((2, 4)),
             dma((2, 8)),
-            dma,
-            dma,
+            dma((2,)),
+            dma((2,)),
             dma,
             dma((2,)),
             dma,

time: 107 us -> 105 us (0.981)
    pallas_call x1, Pallas kernels: 104 us -> 103 us  [per_device(): pl.pallas_call(kernel, out_shape=(jax.ShapeDtypeStruct((TOKENS, D), BF),...]
where the time goes in v5:
time: 105 us
  Pallas kernels  105 us (100%)
    pallas_call x1, Pallas kernels, per_device(): pl.pallas_call(kernel, out_shape=(jax.ShapeDtypeStruct((TOKENS, D), BF),...  103 us

profile of v5, /device:TPU:1, one launch (start us, length us, event | category | flops | bytes accessed | tf_op | source)
XLA Modules:
  0.0 105.1 jit_solution(9906866949130191435)
XLA Ops:
  0.6 102.7 %shard_map.157 = (bf16[16,2048]{1,0:T(8,128)(2,1)}, f32[128,640]{1,0:T(8,128)}) custom-call(bf16[128,512]{1,0:T(8,128)(2,1)} %attn_hbm.1, bf16[512,2048]{1,0:T(8,128)(2,1)} %ow_hbm.1, bf16[16,2048]{1,0:T(8,128)(2,1)} %res_ref.1, f32[1,2048]{1,0:T(1,128)} %bitcast.10, s32[8,128]{1,0:T(8,128)} %bitcast.12, f32[8,128]{1,0:T(8,128)} %bitcast.13, ...), custom_call_target="tpu_custom_call" | custom-call | tf_op jit(solution)/shard_map/pallas_call | solution.py:715
  103.4 1.8 %shard_map.158 = (bf16[16,2048]{1,0:T(8,128)(2,1)}, bf16[128,512]{1,0:T(8,128)(2,1)}, bf16[128,128]{1,0:T(8,128)(2,1)}) custom-call(bf16[16,2048]{1,0:T(8,128)(2,1)} %get-tuple-element.5.moved_ref, f32[128,640]{1,0:T(8,128)} %get-tuple-element.6.raw_ref, f32[1,128]{1,0:T(1,128)} %bitcast.14, f32[1,128]{1,0:T(1,128)} %bitcast.15), custom_call_target="tpu_custom_call" | custom-call | tf_op jit(solution)/shard_map/pallas_call | solution.py:821
